TPU v7x, 32 devices: a whole 2x2x4 slice. The times are simulated.
32 devices in a mesh: blk: 16 (over z, y, core), tp: 2 (over x).
Axes of the slice: x: 2, y: 2, z: 4, core: 2. Of those that a mesh axis runs over, the one named last changes fastest.
Arguments:
- frames: bfloat16 [4096, 1024], P('blk'), may hold values from -6 to 6
- clip_lengths: int32 [8], replicated, may hold values from 1 to 3841, 4096 in all
- text_states: bfloat16 [128, 1024], replicated, may hold values from -6 to 6
- text_segments: int32 [128], replicated, may hold values from 0 to 7, never falling along the last dimension, each value on 1 to 32 neighbouring positions
- gain_one: float32 [1024], replicated, may hold values from 0.1 to 1.9
- shift_one: float32 [1024], replicated, may hold values from -1.5 to 1.5
- gain_two: float32 [1024], replicated, may hold values from 0.1 to 1.9
- shift_two: float32 [1024], replicated, may hold values from -1.5 to 1.5
- gain_three: float32 [1024], replicated, may hold values from 0.1 to 1.9
- shift_three: float32 [1024], replicated, may hold values from -1.5 to 1.5
- query_weight: bfloat16 [1024, 1024], P(None, 'tp'), may hold values from -0.1875 to 0.1875
- key_weight: bfloat16 [1024, 1024], P(None, 'tp'), may hold values from -0.1875 to 0.1875
- value_weight: bfloat16 [1024, 1024], P(None, 'tp'), may hold values from -0.1875 to 0.1875
- output_weight: bfloat16 [1024, 1024], P('tp'), may hold values from -0.75 to 0.75
- cross_query: bfloat16 [1024, 1024], P(None, 'tp'), may hold values from -0.1875 to 0.1875
- cross_key: bfloat16 [1024, 1024], P(None, 'tp'), may hold values from -0.1875 to 0.1875
- cross_value: bfloat16 [1024, 1024], P(None, 'tp'), may hold values from -0.1875 to 0.1875
- cross_output: bfloat16 [1024, 1024], P('tp'), may hold values from -0.375 to 0.375
- inner_weight: bfloat16 [1024, 4096], P(None, 'tp'), may hold values from -0.1875 to 0.1875
- outer_weight: bfloat16 [4096, 1024], P('tp'), may hold values from -0.09375 to 0.09375
- cotangent: bfloat16 [4096, 1024], P('blk'), may hold values from -6 to 6
Outputs:
- result: bfloat16 [4096, 1024], P('blk')
- grad_frames: bfloat16 [4096, 1024], P('blk')
- grad_text: float32 [128, 1024], replicated
- grad_gain_one: float32 [1024], replicated
- grad_shift_one: float32 [1024], replicated
- grad_gain_two: float32 [1024], replicated
- grad_shift_two: float32 [1024], replicated
- grad_gain_three: float32 [1024], replicated
- grad_shift_three: float32 [1024], replicated
- grad_query_weight: float32 [1024, 1024], P(None, 'tp')
- grad_key_weight: float32 [1024, 1024], P(None, 'tp')
- grad_value_weight: float32 [1024, 1024], P(None, 'tp')
- grad_output_weight: float32 [1024, 1024], P('tp')
- grad_cross_query: float32 [1024, 1024], P(None, 'tp')
- grad_cross_key: float32 [1024, 1024], P(None, 'tp')
- grad_cross_value: float32 [1024, 1024], P(None, 'tp')
- grad_cross_output: float32 [1024, 1024], P('tp')
- grad_inner_weight: float32 [1024, 4096], P(None, 'tp')
- grad_outer_weight: float32 [4096, 1024], P('tp')
Inputs may be any that keep to these rules, and one draw needn't show every extreme that they name: `clip_lengths`: clips follow one another in the pack; one of them has 3841 frames. `text_segments`: text tokens of a clip stand together and in clip order; every clip has 1 to 32 of them, one exactly 32.
All inputs are finite; a program needn't handle non-finite values.
Results may differ from a plain program's by a relative error of at most 0.028.
Values may be sent and summed in bfloat16 or wider, within the bound.
No kernel may reach another device: no remote copies, remote signals or barrier semaphores. Data moves between devices by JAX's collectives and lax.ppermute only.
A program may use at most 384 MiB of HBM per device.

v0:
```python
import jax
import jax.numpy as jnp
from jax import lax
from jax.sharding import PartitionSpec as P

HEAD_DIM = 64
EPSILON = 1e-05
NEGATIVE = -1e30


def shifted(block, axis, distance):
    devices = range(lax.axis_size(axis))
    route = [(i - distance, i) for i in devices if i - distance in devices]
    return lax.ppermute(block, axis, route)


def shifted_2(value, axis, by):
    size = lax.axis_size(axis)
    return lax.ppermute(value, axis, [(i, (i + by) % size) for i in range(size)])


def layer_norm(values, gain, shift):
    centre = values - jnp.mean(values, axis=-1, keepdims=True)
    spread = jnp.mean(centre * centre, axis=-1, keepdims=True)
    return centre * lax.rsqrt(spread + EPSILON) * gain + shift


def norm_grads(values, gain, shift, grad):
    _, pullback = jax.vjp(layer_norm, values, gain, shift)
    return pullback(grad)


def gelu_exact(values):
    return jax.nn.gelu(values, approximate=False)


def clip_rows(positions, clip_lengths):
    ends = jnp.cumsum(clip_lengths)
    starts = ends - clip_lengths
    segment = jnp.sum((positions[:, None] >= ends[None, :]).astype(jnp.int32), axis=1)
    match = segment[:, None] == jnp.arange(clip_lengths.shape[0], dtype=jnp.int32)[None, :]
    first = jnp.sum(jnp.where(match, starts[None, :], 0), axis=1)
    return (segment, first)


def matmul(left, right):
    return jnp.dot(left, right, preferred_element_type=jnp.float32)


def head_sum(values):
    return lax.psum(values.astype(jnp.bfloat16), "tp").astype(jnp.float32)


def unchanged(state):
    return state


def block_grads(
    query_heads,
    grad_heads,
    log_total,
    delta,
    query_rows,
    query_first,
    key_heads,
    value_heads,
    key_rows,
):
    allowed = (key_rows[None, :] <= query_rows[:, None]) & (
        key_rows[None, :] >= query_first[:, None]
    )
    score = jnp.einsum("qhd,khd->hqk", query_heads, key_heads, preferred_element_type=jnp.float32)
    weights = jnp.exp(jnp.where(allowed[None], score - log_total[:, :, None], NEGATIVE))
    grad_weights = jnp.einsum(
        "qhd,khd->hqk", grad_heads, value_heads, preferred_element_type=jnp.float32
    )
    grad_score = (weights * (grad_weights - delta[:, :, None])).astype(jnp.bfloat16)
    query_part = jnp.einsum(
        "hqk,khd->qhd", grad_score, key_heads, preferred_element_type=jnp.float32
    )
    key_part = jnp.einsum(
        "hqk,qhd->khd", grad_score, query_heads, preferred_element_type=jnp.float32
    )
    value_part = jnp.einsum(
        "hqk,qhd->khd", weights.astype(jnp.bfloat16), grad_heads, preferred_element_type=jnp.float32
    )
    return (query_part, key_part, value_part)


def shards(
    frames,
    clip_lengths,
    text_states,
    text_segments,
    gain_one,
    shift_one,
    gain_two,
    shift_two,
    gain_three,
    shift_three,
    query_weight,
    key_weight,
    value_weight,
    output_weight,
    cross_query,
    cross_key,
    cross_value,
    cross_output,
    inner_weight,
    outer_weight,
    cotangent,
):
    row_count = frames.shape[0]
    text_count = text_states.shape[0]
    width_here = query_weight.shape[1]
    heads_here = width_here // HEAD_DIM
    blk_count = lax.axis_size("blk")
    blk_index = lax.axis_index("blk")
    scale = float(HEAD_DIM) ** (-0.5)
    my_first_row = blk_index * row_count
    offsets = jnp.arange(row_count, dtype=jnp.int32)
    rows = my_first_row + offsets
    segment, first = clip_rows(rows, clip_lengths)
    inputs = frames.astype(jnp.float32)
    normed_one = layer_norm(inputs, gain_one, shift_one).astype(jnp.bfloat16)
    queries = (matmul(normed_one, query_weight) * scale).astype(jnp.bfloat16)
    keys = matmul(normed_one, key_weight).astype(jnp.bfloat16)
    values = matmul(normed_one, value_weight).astype(jnp.bfloat16)
    query_heads = queries.reshape(row_count, heads_here, HEAD_DIM)
    start_state = (
        jnp.zeros((row_count, heads_here, HEAD_DIM), jnp.float32),
        jnp.full((heads_here, row_count), NEGATIVE, jnp.float32),
        jnp.zeros((heads_here, row_count), jnp.float32),
    )
    start = jnp.int32(0)
    key_piece = lax.all_gather(keys, "blk", axis=0, tiled=True)
    value_piece = lax.all_gather(values, "blk", axis=0, tiled=True)
    count = key_piece.shape[0]
    key_rows = jnp.arange(count, dtype=jnp.int32)

    def fold_work(state):
        totals, run_max, run_sum = state
        piece_keys = key_piece.reshape(count, heads_here, HEAD_DIM)
        piece_values = value_piece.reshape(count, heads_here, HEAD_DIM)
        score = jnp.einsum(
            "qhd,khd->hqk", query_heads, piece_keys, preferred_element_type=jnp.float32
        )
        allowed = (key_rows[None, :] <= rows[:, None]) & (key_rows[None, :] >= first[:, None])
        masked = jnp.where(allowed[None], score, NEGATIVE)
        new_max = jnp.maximum(run_max, jnp.max(masked, axis=-1))
        expo = jnp.where(allowed[None], jnp.exp(masked - new_max[:, :, None]), 0.0)
        run_sum = jnp.sum(expo, axis=-1)
        added = jnp.einsum(
            "hqk,khd->qhd",
            expo.astype(jnp.bfloat16),
            piece_values,
            preferred_element_type=jnp.float32,
        )
        totals = added
        return (totals, new_max, run_sum)

    needed = (start <= rows[-1]) & (start + count - 1 >= first[0])
    totals, run_max, run_sum = lax.cond(needed, fold_work, unchanged, start_state)
    self_out = totals / jnp.transpose(run_sum)[:, :, None]
    log_total = run_max + jnp.log(run_sum)
    attended = self_out.reshape(row_count, width_here).astype(jnp.bfloat16)
    first_sum = inputs + head_sum(matmul(attended, output_weight))
    normed_two = layer_norm(first_sum, gain_two, shift_two).astype(jnp.bfloat16)
    cross_queries = (matmul(normed_two, cross_query) * scale).astype(jnp.bfloat16)
    text_keys = matmul(text_states, cross_key).astype(jnp.bfloat16)
    text_values = matmul(text_states, cross_value).astype(jnp.bfloat16)
    cross_heads = cross_queries.reshape(row_count, heads_here, HEAD_DIM)
    text_key_heads = text_keys.reshape(text_count, heads_here, HEAD_DIM)
    text_value_heads = text_values.reshape(text_count, heads_here, HEAD_DIM)
    allowed_text = segment[:, None] == text_segments[None, :]
    cross_score = jnp.einsum(
        "qhd,khd->hqk", cross_heads, text_key_heads, preferred_element_type=jnp.float32
    )
    cross_masked = jnp.where(allowed_text[None], cross_score, NEGATIVE)
    cross_max = jnp.max(cross_masked, axis=-1, keepdims=True)
    cross_expo = jnp.where(allowed_text[None], jnp.exp(cross_masked - cross_max), 0.0)
    cross_weights = cross_expo / jnp.sum(cross_expo, axis=-1, keepdims=True)
    cross_weights_low = cross_weights.astype(jnp.bfloat16)
    cross_out = jnp.einsum(
        "hqk,khd->qhd", cross_weights_low, text_value_heads, preferred_element_type=jnp.float32
    )
    crossed = cross_out.reshape(row_count, width_here).astype(jnp.bfloat16)
    second_sum = first_sum + head_sum(matmul(crossed, cross_output))
    normed_three = layer_norm(second_sum, gain_three, shift_three).astype(jnp.bfloat16)
    hidden_pre = matmul(normed_three, inner_weight)
    hidden = gelu_exact(hidden_pre).astype(jnp.bfloat16)
    output = second_sum + head_sum(matmul(hidden, outer_weight))
    grad_output = cotangent.astype(jnp.float32)
    grad_outer = matmul(hidden.T, cotangent)
    grad_hidden = matmul(cotangent, outer_weight.T)
    _, gelu_back = jax.vjp(gelu_exact, hidden_pre)
    grad_pre = gelu_back(grad_hidden)[0].astype(jnp.bfloat16)
    grad_inner = matmul(normed_three.T, grad_pre)
    grad_normed_three = head_sum(matmul(grad_pre, inner_weight.T))
    through_three, grad_gain_three, grad_shift_three = norm_grads(
        second_sum, gain_three, shift_three, grad_normed_three
    )
    grad_second = grad_output + through_three
    grad_second_low = grad_second.astype(jnp.bfloat16)
    grad_cross_output = matmul(crossed.T, grad_second_low)
    grad_crossed = (
        matmul(grad_second_low, cross_output.T)
        .astype(jnp.bfloat16)
        .reshape(row_count, heads_here, HEAD_DIM)
    )
    grad_cross_weights = jnp.einsum(
        "qhd,khd->hqk", grad_crossed, text_value_heads, preferred_element_type=jnp.float32
    )
    cross_delta = jnp.transpose(jnp.sum(grad_crossed.astype(jnp.float32) * cross_out, axis=-1))
    grad_cross_score = (cross_weights * (grad_cross_weights - cross_delta[:, :, None])).astype(
        jnp.bfloat16
    )
    grad_cross_heads = jnp.einsum(
        "hqk,khd->qhd", grad_cross_score, text_key_heads, preferred_element_type=jnp.float32
    ).astype(jnp.bfloat16)
    grad_cross_queries = (grad_cross_heads * scale).reshape(row_count, width_here)
    text_key_part = jnp.einsum(
        "hqk,qhd->khd", grad_cross_score, cross_heads, preferred_element_type=jnp.float32
    )
    text_value_part = jnp.einsum(
        "hqk,qhd->khd", cross_weights_low, grad_crossed, preferred_element_type=jnp.float32
    )
    grad_text_keys, grad_text_values = lax.psum(
        (
            text_key_part.reshape(text_count, width_here),
            text_value_part.reshape(text_count, width_here),
        ),
        "blk",
    )
    grad_text_keys = grad_text_keys.astype(jnp.bfloat16)
    grad_text_values = grad_text_values.astype(jnp.bfloat16)
    grad_cross_key = matmul(text_states.T, grad_text_keys)
    grad_cross_value = matmul(text_states.T, grad_text_values)
    grad_text = lax.psum(
        (matmul(grad_text_keys, cross_key.T) + matmul(grad_text_values, cross_value.T)).astype(
            jnp.bfloat16
        ),
        "tp",
    ).astype(jnp.float32)
    grad_cross_query = matmul(normed_two.T, grad_cross_queries)
    grad_normed_two = head_sum(matmul(grad_cross_queries, cross_query.T))
    through_two, grad_gain_two, grad_shift_two = norm_grads(
        first_sum, gain_two, shift_two, grad_normed_two
    )
    grad_first = grad_second + through_two
    grad_first_low = grad_first.astype(jnp.bfloat16)
    grad_output_weight = matmul(attended.T, grad_first_low)
    grad_attended = matmul(grad_first_low, output_weight.T).astype(jnp.bfloat16)
    grad_heads = grad_attended.reshape(row_count, heads_here, HEAD_DIM)
    self_delta = jnp.transpose(jnp.sum(grad_heads.astype(jnp.float32) * self_out, axis=-1))
    zero_block = jnp.zeros((row_count, width_here), jnp.float32)

    def key_turn(turn, carry):
        source = (blk_index - turn) % blk_count
        base = source * row_count

        def key_work(state):
            key_block, value_block, key_grad, value_grad, query_grad = state
            query_part, key_part, value_part = block_grads(
                query_heads,
                grad_heads,
                log_total,
                self_delta,
                rows,
                first,
                key_block.reshape(row_count, heads_here, HEAD_DIM),
                value_block.reshape(row_count, heads_here, HEAD_DIM),
                base + offsets,
            )
            return (
                key_block,
                value_block,
                key_grad + key_part.reshape(row_count, width_here),
                value_grad + value_part.reshape(row_count, width_here),
                query_grad + query_part.reshape(row_count, width_here),
            )

        needed = (base <= rows[-1]) & (base + row_count - 1 >= first[0])
        key_block, value_block, key_grad, value_grad, query_grad = lax.cond(
            needed, key_work, unchanged, carry
        )
        key_block, value_block = shifted((key_block, value_block), "blk", 1)
        key_grad, value_grad = (
            shifted_2(key_grad.astype(jnp.bfloat16), "blk", 1).astype(key_grad.dtype),
            shifted_2(value_grad.astype(jnp.bfloat16), "blk", 1).astype(value_grad.dtype),
        )
        return (key_block, value_block, key_grad, value_grad, query_grad)

    final = lax.fori_loop(
        0, blk_count, key_turn, (keys, values, zero_block, zero_block, zero_block)
    )
    key_total, value_total, query_total = (final[2], final[3], final[4])
    grad_queries = query_total.astype(jnp.bfloat16) * scale
    grad_keys = key_total.astype(jnp.bfloat16)
    grad_values = value_total.astype(jnp.bfloat16)
    grad_query_weight = matmul(normed_one.T, grad_queries)
    grad_key_weight = matmul(normed_one.T, grad_keys)
    grad_value_weight = matmul(normed_one.T, grad_values)
    grad_normed_one = head_sum(
        matmul(grad_queries, query_weight.T)
        + matmul(grad_keys, key_weight.T)
        + matmul(grad_values, value_weight.T)
    )
    through_one, grad_gain_one, grad_shift_one = norm_grads(
        inputs, gain_one, shift_one, grad_normed_one
    )
    grad_frames = (grad_first + through_one).astype(jnp.bfloat16)
    (
        grad_query_weight,
        grad_key_weight,
        grad_value_weight,
        grad_output_weight,
        grad_cross_query,
        grad_cross_output,
        grad_inner,
        grad_outer,
        grad_gain_one,
        grad_shift_one,
        grad_gain_two,
        grad_shift_two,
        grad_gain_three,
        grad_shift_three,
    ) = lax.psum(
        (
            grad_query_weight,
            grad_key_weight,
            grad_value_weight,
            grad_output_weight,
            grad_cross_query,
            grad_cross_output,
            grad_inner,
            grad_outer,
            grad_gain_one,
            grad_shift_one,
            grad_gain_two,
            grad_shift_two,
            grad_gain_three,
            grad_shift_three,
        ),
        "blk",
    )
    return (
        output.astype(jnp.bfloat16),
        grad_frames,
        grad_text,
        grad_gain_one,
        grad_shift_one,
        grad_gain_two,
        grad_shift_two,
        grad_gain_three,
        grad_shift_three,
        grad_query_weight,
        grad_key_weight,
        grad_value_weight,
        grad_output_weight,
        grad_cross_query,
        grad_cross_key,
        grad_cross_value,
        grad_cross_output,
        grad_inner,
        grad_outer,
    )


def solution(mesh):
    return jax.shard_map(
        shards,
        mesh=mesh,
        in_specs=(
            P("blk", None),
            P(),
            P(),
            P(),
            P(),
            P(),
            P(),
            P(),
            P(),
            P(),
            P(None, "tp"),
            P(None, "tp"),
            P(None, "tp"),
            P("tp", None),
            P(None, "tp"),
            P(None, "tp"),
            P(None, "tp"),
            P("tp", None),
            P(None, "tp"),
            P("tp", None),
            P("blk", None),
        ),
        out_specs=(
            P("blk", None),
            P("blk", None),
            P(),
            P(),
            P(),
            P(),
            P(),
            P(),
            P(),
            P(None, "tp"),
            P(None, "tp"),
            P(None, "tp"),
            P("tp", None),
            P(None, "tp"),
            P(None, "tp"),
            P(None, "tp"),
            P("tp", None),
            P(None, "tp"),
            P("tp", None),
        ),
        check_vma=False,
    )
```

profile of v0, /device:TPU:0, one launch (start us, length us, event | category | flops | bytes accessed | tf_op | source)
XLA Modules:
  0.0 1468.9 jit_solution(12834105977165518617)
XLA Ops:
  21.8 44.2 %all-gather.3.cloned.1.call-done = bf16[4096,512]{1,0:T(8,128)(2,1)} async-done(((bf16[256,512]{1,0:T(8,128)(2,1)}), bf16[4096,512]{1,0:T(8,128)(2,1)}) %all-gather.3.cloned.1.call-update) | async-done | bytes 4194320 | tf_op jit(solution)/shard_map/all_gather | solution.py:136
  66.1 51.8 %all-gather.5.cloned.1.call-done = bf16[4096,512]{1,0:T(8,128)(2,1)} async-done(((bf16[256,512]{1,0:T(8,128)(2,1)}), bf16[4096,512]{1,0:T(8,128)(2,1)}) %all-gather.5.cloned.1.call-update) | async-done | bytes 4194320 | tf_op jit(solution)/shard_map/all_gather | solution.py:137
  117.9 62.9 %conditional.2 = (f32[256,8,64]{0,2,1:T(8,128)S(1)}, f32[8,256]{1,0:T(8,128)}, f32[8,256]{1,0:T(8,128)}, f32[8,256]{1,0:T(8,128)S(1)}) conditional(s32[]{:T(128)} %bitcast.13, () %tuple.55, (s32[4096]{0:T(1024)S(1)}, s32[4096]{0:T(1024)S(1)}, s32[256]{0:T(256)}, s32[256]{0:T(256)}, bf16[4096,512]{1,0:T(8,128)(2,1)}, ...), branch_computations={%region_5.6_spmd, %region_6.9_spmd} | conditional | flops 2234513408 | bytes 130910240 | solution.py:163
  117.9 6.3 copy.81
  125.8 6.3 copy.80
  132.2 15.7 %select_reduce_fusion = (f32[8,256]{1,0:T(8,128)S(1)}, f32[8,256,4096]{2,1,0:T(8,128)}) fusion(pred[256,4096]{1,0:T(8,128)(4,1)S(1)} %compare_and_fusion, bf16[256,8,64]{0,2,1:T(8,128)(2,1)S(1)} %get-tuple-element.475, bf16[4096,8,64]{0,2,1:T(8,128)(2,1)} %bitcast.126), kind=kOutput, calls=%fused_computation.2 | convolution fusion | flops 1090516992 | bytes 39067648 | tf_op jit(solution)/shard_map/cond/branch_1_fun/qhd,khd->hqk/dot_general | solution.py:145
  148.4 15.5 %fusion.7 = f32[256,8,64]{0,2,1:T(8,128)S(1)} fusion(bf16[4096,8,64]{0,2,1:T(8,128)(2,1)} %bitcast.133, f32[8,256,4096]{2,1,0:T(8,128)} %get-tuple-element.768, f32[8,256]{1,0:T(8,128)} %broadcast_maximum_fusion, pred[256,4096]{1,0:T(8,128)(4,1)S(1)} %compare_and_fusion), kind=kOutput, calls=%fused_computation.8 | convolution fusion | flops 1107296256 | bytes 39329792 | tf_op jit(solution)/shard_map/cond/branch_1_fun/hqk,khd->qhd/dot_general | solution.py:153
  163.9 16.2 %fusion.2 = f32[8,256]{1,0:T(8,128)} fusion(f32[8,256,4096]{2,1,0:T(8,128)} %get-tuple-element.768, f32[8,256]{1,0:T(8,128)} %broadcast_maximum_fusion, pred[256,4096]{1,0:T(8,128)(4,1)S(1)} %compare_and_fusion), kind=kLoop, calls=%fused_computation.3 | loop fusion | flops 33552384 | bytes 34619392 | tf_op jit(solution)/shard_map/cond/branch_1_fun/reduce_sum | solution.py:152
  189.6 21.9 %all-reduce.12.cloned.1.call-done = bf16[256,1024]{1,0:T(8,128)(2,1)} async-done(((bf16[256,1024]{1,0:T(8,128)(2,1)}), bf16[256,1024]{1,0:T(8,128)(2,1)}) %all-reduce.12.cloned.1.call-update) | async-done | bytes 524304 | tf_op jit(solution)/shard_map/psum | solution.py:51
  228.4 25.3 %all-reduce.14.cloned.1.call-done = bf16[256,1024]{1,0:T(8,128)(2,1)} async-done(((bf16[256,1024]{1,0:T(8,128)(2,1)}), bf16[256,1024]{1,0:T(8,128)(2,1)}) %all-reduce.14.cloned.1.call-update) | async-done | bytes 524304 | tf_op jit(solution)/shard_map/psum | solution.py:51
  256.5 3.7 fusion.86
  260.2 6.6 add_convert_fusion
  271.9 6.2 fusion.105
  280.3 4.8 fusion.85
  285.1 15.5 %all-reduce.16.cloned.1.call-done = bf16[256,1024]{1,0:T(8,128)(2,1)} async-done(((bf16[256,1024]{1,0:T(8,128)(2,1)}), bf16[256,1024]{1,0:T(8,128)(2,1)}) %all-reduce.16.cloned.1.call-update) | async-done | bytes 524304 | tf_op jit(solution)/shard_map/psum | solution.py:51
  317.8 25.6 %all-reduce.18.cloned.1.call-done = bf16[256,1024]{1,0:T(8,128)(2,1)} async-done(((bf16[256,1024]{1,0:T(8,128)(2,1)}), bf16[256,1024]{1,0:T(8,128)(2,1)}) %all-reduce.18.cloned.1.call-update) | async-done | bytes 524304 | tf_op jit(solution)/shard_map/psum | solution.py:51
  353.3 421.7 %while.26 = (s32[]{:T(128)}, bf16[256,512]{0,1:T(8,128)(2,1)S(1)}, bf16[256,512]{0,1:T(8,128)(2,1)}, f32[256,512]{0,1:T(8,128)}, f32[256,512]{0,1:T(8,128)}, /*i...) while((s32[]{:T(128)}, bf16[256,512]{0,1:T(8,128)(2,1)S(1)}, ...), condition=%wide.region_29.30_spmd.clone, body=%wide.region_26.29_spmd.clone.sunk | while | flops 341115168 | bytes 37714808 | solution.py:294
  359.2 5.0 conditional.5
  368.5 3.5 collective-permute-start.1
  384.2 6.3 collective-permute-start.2
  395.5 4.4 collective-permute-start.1
  413.3 7.3 collective-permute-start.3
  422.6 5.2 collective-permute-start.1
  443.0 7.5 collective-permute-start
  450.5 5.2 collective-permute-start.1
  473.5 10.1 collective-permute-start.1
  501.4 5.2 collective-permute-start.1
  525.6 5.2 collective-permute-start.1
  543.6 6.3 collective-permute-start.3
  549.9 3.6 collective-permute-start
  553.5 5.2 collective-permute-start.1
  573.9 7.4 collective-permute-start
  581.3 5.2 collective-permute-start.1
  604.4 9.1 collective-permute-start.1
  632.3 5.2 collective-permute-start.1
  656.4 5.2 collective-permute-start.1
  674.5 5.3 collective-permute-start.3
  679.7 4.6 collective-permute-start
  684.3 5.2 collective-permute-start.1
  704.7 7.4 collective-permute-start
  712.2 5.2 collective-permute-start.1
  735.2 8.1 collective-permute-start.1
  763.1 5.2 collective-permute-start.1
  784.6 31.8 %all-reduce.20.cloned.1.call-done = bf16[256,1024]{1,0:T(8,128)(2,1)} async-done(((bf16[256,1024]{1,0:T(8,128)(2,1)}), bf16[256,1024]{1,0:T(8,128)(2,1)}) %all-reduce.20.cloned.1.call-update) | async-done | bytes 524304 | tf_op jit(solution)/shard_map/psum | solution.py:51
  820.2 67.9 %all-reduce.25 = (bf16[128,512]{0,1:T(8,128)(2,1)S(1)}, bf16[128,512]{0,1:T(8,128)(2,1)}, f32[1024]{0:T(1024)}, f32[1024]{0:T(1024)}, f32[1024]{0:T(1024)}, /*in...) all-reduce(f32[128,512]{0,1:T(8,128)S(1)} %bitcast.142, ...), channel_id=1, replica_groups=mesh['blk'=16,'tp'=2] {'blk'}, use_global_device_ids=true, to_apply=%region_33.34 | all-reduce | flops 137216 | bytes 835584 | tf_op jit(solution)/shard_map/psum | solution.py:228
  909.3 13.6 all-reduce.24.cloned.1.call-done
  926.7 512.8 %all-reduce.22.cloned.1.call-done = (f32[1024,512]{1,0:T(8,128)}, f32[1024,512]{1,0:T(8,128)}, f32[1024,512]{1,0:T(8,128)}, f32[512,1024]{1,0:T(8,128)}, f32[102...) async-done(((f32[1024,512]{1,0:T(8,128)}, f32[1024,512]{1,0:T(8,128)}, f32[1024,512]{1,0:T(8,128)}, f32[512,1024]{1,0:T(8,128)}, ...) | async-done | bytes 29360144 | tf_op jit(solution)/shard_map/psum | solution.py:328
  1453.1 4.3 copy.164
  (696 shorter events, 385.8 us)
Async XLA Ops:
  7.3 58.8 %all-gather.3.cloned.1.call-start = ((), (), s32[]{:S(2)}) async-start(), calls=%async_computation | async-start | bytes 4456448 | tf_op jit(solution)/shard_map/all_gather | solution.py:136
  12.7 105.2 %all-gather.5.cloned.1.call-start = ((), (), s32[]{:S(2)}) async-start(), calls=%async_computation.1 | async-start | bytes 4456448 | tf_op jit(solution)/shard_map/all_gather | solution.py:137
  14.0 197.5 %all-reduce.12.cloned.1.call-start = ((), (), s32[]{:S(2)}) async-start(), calls=%async_computation.2 | async-start | bytes 1048576 | tf_op jit(solution)/shard_map/psum | solution.py:51
  184.3 69.4 %all-reduce.14.cloned.1.call-start = ((), (), s32[]{:S(2)}) async-start(), calls=%async_computation.3 | async-start | bytes 1048576 | tf_op jit(solution)/shard_map/psum | solution.py:51
  224.9 75.7 %all-reduce.16.cloned.1.call-start = ((), (), s32[]{:S(2)}) async-start(), calls=%async_computation.4 | async-start | bytes 1048576 | tf_op jit(solution)/shard_map/psum | solution.py:51
  271.9 71.5 %all-reduce.18.cloned.1.call-start = ((), (), s32[]{:S(2)}) async-start(), calls=%async_computation.5 | async-start | bytes 1048576 | tf_op jit(solution)/shard_map/psum | solution.py:51
  314.6 501.9 %all-reduce.20.cloned.1.call-start = ((), (), s32[]{:S(2)}) async-start(), calls=%async_computation.6 | async-start | bytes 1048576 | tf_op jit(solution)/shard_map/psum | solution.py:51
  384.2 15.7 %collective-permute-start.2 = (bf16[256,512]{0,1:T(8,128)(2,1)S(1)}, bf16[256,512]{0,1:T(8,128)(2,1)}, u32[]{:S(2)}, u32[]{:S(2)}) collective-permute-start(bf16[256,512]{0,1:T(8,128)(2,1)S(1)} %convert_element_type.500), channel_id=1, source_target_pairs={{0,2},{2,4},{4,6},{6,8},{8,10},{10,12},{12,14},{14,16},{16,18},{18... | collective-permute-start | bytes 786440 | tf_op jit(solution)/shard_map/while/body/eval_jaxpr/ppermute | solution.py:19
  410.3 17.5 %collective-permute-start.2 = (bf16[256,512]{0,1:T(8,128)(2,1)S(1)}, bf16[256,512]{0,1:T(8,128)(2,1)}, u32[]{:S(2)}, u32[]{:S(2)}) collective-permute-start(bf16[256,512]{0,1:T(8,128)(2,1)S(1)} %convert_element_type.500), channel_id=1, source_target_pairs={{0,2},{2,4},{4,6},{6,8},{8,10},{10,12},{12,14},{14,16},{16,18},{18... | collective-permute-start | bytes 786440 | tf_op jit(solution)/shard_map/while/body/eval_jaxpr/ppermute | solution.py:19
  413.3 16.3 %collective-permute-start.3 = (bf16[256,512]{0,1:T(8,128)(2,1)}, bf16[256,512]{0,1:T(8,128)(2,1)S(1)}, u32[]{:S(2)}, u32[]{:S(2)}) collective-permute-start(bf16[256,512]{0,1:T(8,128)(2,1)} %convert_element_type.502), channel_id=1, source_target_pairs={{0,2},{2,4},{4,6},{6,8},{8,10},{10,12},{12,14},{14,16},{16,18},{18... | collective-permute-start | bytes 786440 | tf_op jit(solution)/shard_map/while/body/eval_jaxpr/ppermute | solution.py:19
  438.2 17.5 %collective-permute-start.2 = (bf16[256,512]{0,1:T(8,128)(2,1)S(1)}, bf16[256,512]{0,1:T(8,128)(2,1)}, u32[]{:S(2)}, u32[]{:S(2)}) collective-permute-start(bf16[256,512]{0,1:T(8,128)(2,1)S(1)} %convert_element_type.500), channel_id=1, source_target_pairs={{0,2},{2,4},{4,6},{6,8},{8,10},{10,12},{12,14},{14,16},{16,18},{18... | collective-permute-start | bytes 786440 | tf_op jit(solution)/shard_map/while/body/eval_jaxpr/ppermute | solution.py:19
  440.7 16.8 %collective-permute-start.3 = (bf16[256,512]{0,1:T(8,128)(2,1)}, bf16[256,512]{0,1:T(8,128)(2,1)S(1)}, u32[]{:S(2)}, u32[]{:S(2)}) collective-permute-start(bf16[256,512]{0,1:T(8,128)(2,1)} %convert_element_type.502), channel_id=1, source_target_pairs={{0,2},{2,4},{4,6},{6,8},{8,10},{10,12},{12,14},{14,16},{16,18},{18... | collective-permute-start | bytes 786440 | tf_op jit(solution)/shard_map/while/body/eval_jaxpr/ppermute | solution.py:19
  443.0 15.3 %collective-permute-start = (bf16[256,512]{0,1:T(8,128)(2,1)S(1)}, bf16[256,512]{0,1:T(8,128)(2,1)S(1)}, u32[]{:S(2)}, u32[]{:S(2)}) collective-permute-start(bf16[256,512]{0,1:T(8,128)(2,1)S(1)} %copy.126), channel_id=1, source_target_pairs={{0,2},{2,4},{4,6},{6,8},{8,10},{10,12},{12,14},{14,16},{16,18},{18... | collective-permute-start | bytes 786440 | tf_op jit(solution)/shard_map/while/body/eval_jaxpr/ppermute | solution.py:14
  466.1 17.5 %collective-permute-start.2 = (bf16[256,512]{0,1:T(8,128)(2,1)S(1)}, bf16[256,512]{0,1:T(8,128)(2,1)}, u32[]{:S(2)}, u32[]{:S(2)}) collective-permute-start(bf16[256,512]{0,1:T(8,128)(2,1)S(1)} %convert_element_type.500), channel_id=1, source_target_pairs={{0,2},{2,4},{4,6},{6,8},{8,10},{10,12},{12,14},{14,16},{16,18},{18... | collective-permute-start | bytes 786440 | tf_op jit(solution)/shard_map/while/body/eval_jaxpr/ppermute | solution.py:19
  468.6 16.8 %collective-permute-start.3 = (bf16[256,512]{0,1:T(8,128)(2,1)}, bf16[256,512]{0,1:T(8,128)(2,1)S(1)}, u32[]{:S(2)}, u32[]{:S(2)}) collective-permute-start(bf16[256,512]{0,1:T(8,128)(2,1)} %convert_element_type.502), channel_id=1, source_target_pairs={{0,2},{2,4},{4,6},{6,8},{8,10},{10,12},{12,14},{14,16},{16,18},{18... | collective-permute-start | bytes 786440 | tf_op jit(solution)/shard_map/while/body/eval_jaxpr/ppermute | solution.py:19
  470.9 15.3 %collective-permute-start = (bf16[256,512]{0,1:T(8,128)(2,1)S(1)}, bf16[256,512]{0,1:T(8,128)(2,1)S(1)}, u32[]{:S(2)}, u32[]{:S(2)}) collective-permute-start(bf16[256,512]{0,1:T(8,128)(2,1)S(1)} %copy.126), channel_id=1, source_target_pairs={{0,2},{2,4},{4,6},{6,8},{8,10},{10,12},{12,14},{14,16},{16,18},{18... | collective-permute-start | bytes 786440 | tf_op jit(solution)/shard_map/while/body/eval_jaxpr/ppermute | solution.py:14
  473.5 12.7 collective-permute-start.1
  494.0 12.5 collective-permute-start.2
  496.5 11.9 collective-permute-start.3
  517.0 13.8 collective-permute-start.2
  520.6 11.9 collective-permute-start.3
  541.2 17.5 %collective-permute-start.2 = (bf16[256,512]{0,1:T(8,128)(2,1)S(1)}, bf16[256,512]{0,1:T(8,128)(2,1)}, u32[]{:S(2)}, u32[]{:S(2)}) collective-permute-start(bf16[256,512]{0,1:T(8,128)(2,1)S(1)} %convert_element_type.500), channel_id=1, source_target_pairs={{0,2},{2,4},{4,6},{6,8},{8,10},{10,12},{12,14},{14,16},{16,18},{18... | collective-permute-start | bytes 786440 | tf_op jit(solution)/shard_map/while/body/eval_jaxpr/ppermute | solution.py:19
  543.6 16.8 %collective-permute-start.3 = (bf16[256,512]{0,1:T(8,128)(2,1)}, bf16[256,512]{0,1:T(8,128)(2,1)S(1)}, u32[]{:S(2)}, u32[]{:S(2)}) collective-permute-start(bf16[256,512]{0,1:T(8,128)(2,1)} %convert_element_type.502), channel_id=1, source_target_pairs={{0,2},{2,4},{4,6},{6,8},{8,10},{10,12},{12,14},{14,16},{16,18},{18... | collective-permute-start | bytes 786440 | tf_op jit(solution)/shard_map/while/body/eval_jaxpr/ppermute | solution.py:19
  569.1 17.4 %collective-permute-start.2 = (bf16[256,512]{0,1:T(8,128)(2,1)S(1)}, bf16[256,512]{0,1:T(8,128)(2,1)}, u32[]{:S(2)}, u32[]{:S(2)}) collective-permute-start(bf16[256,512]{0,1:T(8,128)(2,1)S(1)} %convert_element_type.500), channel_id=1, source_target_pairs={{0,2},{2,4},{4,6},{6,8},{8,10},{10,12},{12,14},{14,16},{16,18},{18... | collective-permute-start | bytes 786440 | tf_op jit(solution)/shard_map/while/body/eval_jaxpr/ppermute | solution.py:19
  571.5 16.8 %collective-permute-start.3 = (bf16[256,512]{0,1:T(8,128)(2,1)}, bf16[256,512]{0,1:T(8,128)(2,1)S(1)}, u32[]{:S(2)}, u32[]{:S(2)}) collective-permute-start(bf16[256,512]{0,1:T(8,128)(2,1)} %convert_element_type.502), channel_id=1, source_target_pairs={{0,2},{2,4},{4,6},{6,8},{8,10},{10,12},{12,14},{14,16},{16,18},{18... | collective-permute-start | bytes 786440 | tf_op jit(solution)/shard_map/while/body/eval_jaxpr/ppermute | solution.py:19
  573.9 15.2 %collective-permute-start = (bf16[256,512]{0,1:T(8,128)(2,1)S(1)}, bf16[256,512]{0,1:T(8,128)(2,1)S(1)}, u32[]{:S(2)}, u32[]{:S(2)}) collective-permute-start(bf16[256,512]{0,1:T(8,128)(2,1)S(1)} %copy.126), channel_id=1, source_target_pairs={{0,2},{2,4},{4,6},{6,8},{8,10},{10,12},{12,14},{14,16},{16,18},{18... | collective-permute-start | bytes 786440 | tf_op jit(solution)/shard_map/while/body/eval_jaxpr/ppermute | solution.py:14
  597.0 16.5 %collective-permute-start.2 = (bf16[256,512]{0,1:T(8,128)(2,1)S(1)}, bf16[256,512]{0,1:T(8,128)(2,1)}, u32[]{:S(2)}, u32[]{:S(2)}) collective-permute-start(bf16[256,512]{0,1:T(8,128)(2,1)S(1)} %convert_element_type.500), channel_id=1, source_target_pairs={{0,2},{2,4},{4,6},{6,8},{8,10},{10,12},{12,14},{14,16},{16,18},{18... | collective-permute-start | bytes 786440 | tf_op jit(solution)/shard_map/while/body/eval_jaxpr/ppermute | solution.py:19
  599.4 15.9 %collective-permute-start.3 = (bf16[256,512]{0,1:T(8,128)(2,1)}, bf16[256,512]{0,1:T(8,128)(2,1)S(1)}, u32[]{:S(2)}, u32[]{:S(2)}) collective-permute-start(bf16[256,512]{0,1:T(8,128)(2,1)} %convert_element_type.502), channel_id=1, source_target_pairs={{0,2},{2,4},{4,6},{6,8},{8,10},{10,12},{12,14},{14,16},{16,18},{18... | collective-permute-start | bytes 786440 | tf_op jit(solution)/shard_map/while/body/eval_jaxpr/ppermute | solution.py:19
  601.8 14.3 collective-permute-start
  604.4 11.7 collective-permute-start.1
  623.9 13.6 collective-permute-start.2
  627.3 12.0 collective-permute-start.3
  647.9 13.7 collective-permute-start.2
  651.4 12.7 collective-permute-start.3
  672.8 16.7 %collective-permute-start.2 = (bf16[256,512]{0,1:T(8,128)(2,1)S(1)}, bf16[256,512]{0,1:T(8,128)(2,1)}, u32[]{:S(2)}, u32[]{:S(2)}) collective-permute-start(bf16[256,512]{0,1:T(8,128)(2,1)S(1)} %convert_element_type.500), channel_id=1, source_target_pairs={{0,2},{2,4},{4,6},{6,8},{8,10},{10,12},{12,14},{14,16},{16,18},{18... | collective-permute-start | bytes 786440 | tf_op jit(solution)/shard_map/while/body/eval_jaxpr/ppermute | solution.py:19
  674.5 16.8 %collective-permute-start.3 = (bf16[256,512]{0,1:T(8,128)(2,1)}, bf16[256,512]{0,1:T(8,128)(2,1)S(1)}, u32[]{:S(2)}, u32[]{:S(2)}) collective-permute-start(bf16[256,512]{0,1:T(8,128)(2,1)} %convert_element_type.502), channel_id=1, source_target_pairs={{0,2},{2,4},{4,6},{6,8},{8,10},{10,12},{12,14},{14,16},{16,18},{18... | collective-permute-start | bytes 786440 | tf_op jit(solution)/shard_map/while/body/eval_jaxpr/ppermute | solution.py:19
  679.7 12.4 collective-permute-start
  699.9 17.4 %collective-permute-start.2 = (bf16[256,512]{0,1:T(8,128)(2,1)S(1)}, bf16[256,512]{0,1:T(8,128)(2,1)}, u32[]{:S(2)}, u32[]{:S(2)}) collective-permute-start(bf16[256,512]{0,1:T(8,128)(2,1)S(1)} %convert_element_type.500), channel_id=1, source_target_pairs={{0,2},{2,4},{4,6},{6,8},{8,10},{10,12},{12,14},{14,16},{16,18},{18... | collective-permute-start | bytes 786440 | tf_op jit(solution)/shard_map/while/body/eval_jaxpr/ppermute | solution.py:19
  702.4 16.8 %collective-permute-start.3 = (bf16[256,512]{0,1:T(8,128)(2,1)}, bf16[256,512]{0,1:T(8,128)(2,1)S(1)}, u32[]{:S(2)}, u32[]{:S(2)}) collective-permute-start(bf16[256,512]{0,1:T(8,128)(2,1)} %convert_element_type.502), channel_id=1, source_target_pairs={{0,2},{2,4},{4,6},{6,8},{8,10},{10,12},{12,14},{14,16},{16,18},{18... | collective-permute-start | bytes 786440 | tf_op jit(solution)/shard_map/while/body/eval_jaxpr/ppermute | solution.py:19
  704.7 15.2 %collective-permute-start = (bf16[256,512]{0,1:T(8,128)(2,1)S(1)}, bf16[256,512]{0,1:T(8,128)(2,1)S(1)}, u32[]{:S(2)}, u32[]{:S(2)}) collective-permute-start(bf16[256,512]{0,1:T(8,128)(2,1)S(1)} %copy.126), channel_id=1, source_target_pairs={{0,2},{2,4},{4,6},{6,8},{8,10},{10,12},{12,14},{14,16},{16,18},{18... | collective-permute-start | bytes 786440 | tf_op jit(solution)/shard_map/while/body/eval_jaxpr/ppermute | solution.py:14
  727.8 15.5 %collective-permute-start.2 = (bf16[256,512]{0,1:T(8,128)(2,1)S(1)}, bf16[256,512]{0,1:T(8,128)(2,1)}, u32[]{:S(2)}, u32[]{:S(2)}) collective-permute-start(bf16[256,512]{0,1:T(8,128)(2,1)S(1)} %convert_element_type.500), channel_id=1, source_target_pairs={{0,2},{2,4},{4,6},{6,8},{8,10},{10,12},{12,14},{14,16},{16,18},{18... | collective-permute-start | bytes 786440 | tf_op jit(solution)/shard_map/while/body/eval_jaxpr/ppermute | solution.py:19
  730.2 15.3 %collective-permute-start.3 = (bf16[256,512]{0,1:T(8,128)(2,1)}, bf16[256,512]{0,1:T(8,128)(2,1)S(1)}, u32[]{:S(2)}, u32[]{:S(2)}) collective-permute-start(bf16[256,512]{0,1:T(8,128)(2,1)} %convert_element_type.502), channel_id=1, source_target_pairs={{0,2},{2,4},{4,6},{6,8},{8,10},{10,12},{12,14},{14,16},{16,18},{18... | collective-permute-start | bytes 786440 | tf_op jit(solution)/shard_map/while/body/eval_jaxpr/ppermute | solution.py:19
  732.6 13.8 collective-permute-start
  754.2 16.6 %collective-permute-start.2 = (bf16[256,512]{0,1:T(8,128)(2,1)S(1)}, bf16[256,512]{0,1:T(8,128)(2,1)}, u32[]{:S(2)}, u32[]{:S(2)}) collective-permute-start(bf16[256,512]{0,1:T(8,128)(2,1)S(1)} %convert_element_type.500), channel_id=1, source_target_pairs={{0,2},{2,4},{4,6},{6,8},{8,10},{10,12},{12,14},{14,16},{16,18},{18... | collective-permute-start | bytes 786440 | tf_op jit(solution)/shard_map/while/body/eval_jaxpr/ppermute | solution.py:19
  758.1 15.3 %collective-permute-start.3 = (bf16[256,512]{0,1:T(8,128)(2,1)}, bf16[256,512]{0,1:T(8,128)(2,1)S(1)}, u32[]{:S(2)}, u32[]{:S(2)}) collective-permute-start(bf16[256,512]{0,1:T(8,128)(2,1)} %convert_element_type.502), channel_id=1, source_target_pairs={{0,2},{2,4},{4,6},{6,8},{8,10},{10,12},{12,14},{14,16},{16,18},{18... | collective-permute-start | bytes 786440 | tf_op jit(solution)/shard_map/while/body/eval_jaxpr/ppermute | solution.py:19
  760.5 13.8 collective-permute-start
  779.7 143.2 %all-reduce.24.cloned.1.call-start = ((), (), s32[]{:S(2)}) async-start(), calls=%async_computation.8 | async-start | bytes 1572864 | tf_op jit(solution)/shard_map/psum | solution.py:51
  891.9 547.5 %all-reduce.22.cloned.1.call-start = ((), (), s32[]{:S(2)}) async-start(), calls=%async_computation.7 | async-start | bytes 58720256 | tf_op jit(solution)/shard_map/psum | solution.py:328
  (170 other events, 1533.0 us)
Sparse Core Ops, SparseCore 0:
  12.8 53.2 all-gather.2
  68.8 49.0 all-gather.4
  184.4 27.0 all-reduce.11
  225.1 28.5 all-reduce.13
  272.0 28.5 all-reduce.15
  314.7 28.5 all-reduce.17
  779.8 36.5 all-reduce.19
  892.0 30.8 all-reduce.23
  929.9 509.5 all-reduce.21
where the time goes:
time: 1480 us; the launch traced here: 1470 us
  waiting for transfers between devices  749 us (51%)
  starting transfers between devices  234 us (16%)
  local copies, waits for them, and re-layouts  142 us (10%)
  other arithmetic  127 us (9%)
  matrix products  109 us (7%)
  blocking collectives  67.9 us (5%)
  loops' own time  23.5 us (2%)
  between operations  16.3 us (1%)
    psum x1, waiting for transfers between devices, shards(): lax.psum((grad_query_weight, grad_key_weight, grad_value_weight, grad_out...  513 us
    ppermute x32, starting transfers between devices, shifted(): return lax.ppermute(block, axis, route)  149 us
    psum x6, waiting for transfers between devices, head_sum(): return lax.psum(values.astype(jnp.bfloat16), 'tp').astype(jnp.float32)  134 us
    ppermute x32, starting transfers between devices, shifted_2(): lax.ppermute(value, axis, [(i, (i + by) % size) for i in range(size)])  83.7 us
    psum x1, blocking collectives, shards(): lax.psum((text_key_part.reshape(text_count, width_here), text_value_part....  67.9 us
    dot_general x30, matrix products, matmul(): return jnp.dot(left, right, preferred_element_type=jnp.float32)  67 us
    all_gather x1, waiting for transfers between devices, shards(): value_piece = lax.all_gather(values, 'blk', axis=0, tiled=True)  51.8 us
    all_gather x1, waiting for transfers between devices, shards(): key_piece = lax.all_gather(keys, 'blk', axis=0, tiled=True)  44.2 us
  transfers between devices with their start and end apart: 73, of which 15 were waited for; matrix products, arithmetic and copies ran while one was open for 7% of the time, Pallas kernels for 0%

commit v1 on v0

--- a/solution.py
+++ b/solution.py
@@ -6,6 +6,19 @@
 HEAD_DIM = 64
 EPSILON = 1e-05
 NEGATIVE = -1e30
+
+
+def gather_around(array, axis, dim):
+    ways = lax.axis_size(axis)
+    up = [(d, (d + 1) % ways) for d in range(ways)]
+    down = [(d, (d - 1) % ways) for d in range(ways)]
+    earlier, later = ([array], [array])
+    for _ in range(ways // 2):
+        earlier.append(lax.ppermute(earlier[-1], axis, up))
+    for _ in range((ways - 1) // 2):
+        later.append(lax.ppermute(later[-1], axis, down))
+    line = jnp.concatenate([*earlier[::-1], *later[1:]], axis=dim)
+    return jnp.roll(line, (lax.axis_index(axis) - ways // 2) * array.shape[dim], axis=dim)
 
 
 def shifted(block, axis, distance):
@@ -134,7 +147,7 @@
     )
     start = jnp.int32(0)
     key_piece = lax.all_gather(keys, "blk", axis=0, tiled=True)
-    value_piece = lax.all_gather(values, "blk", axis=0, tiled=True)
+    value_piece = gather_around(values, "blk", 0)
     count = key_piece.shape[0]
     key_rows = jnp.arange(count, dtype=jnp.int32)
 

time: 1480 us -> 1470 us (level)
  waiting for transfers between devices: 749 us -> 705 us
  starting transfers between devices: 234 us -> 271 us
    all_gather x1 -> x0, waiting for transfers between devices: 51.8 us -> none  [shards(): value_piece = lax.all_gather(values, 'blk', axis=0, tiled=True)]
    all_gather x1, waiting for transfers between devices: 44.2 us -> 0.01 us  [shards(): key_piece = lax.all_gather(keys, 'blk', axis=0, tiled=True)]
    ppermute x0 -> x15, waiting for transfers between devices: none -> 43.8 us  [the longest x8 37.5 us: gather_around(): earlier.append(lax.ppermute(earlier[-1], axis, up))]
    unnamed x198 -> x231, local copies, waits for them, and re-layouts: 39 us -> 72.8 us
    ppermute x0 -> x15, starting transfers between devices: none -> 31.7 us  [the longest x7 31.2 us: gather_around(): later.append(lax.ppermute(later[-1], axis, down))]
    while x128 -> x32, local copies, waits for them, and re-layouts: 39.7 us -> 11.6 us
    slice x32, local copies, waits for them, and re-layouts: 41.3 us -> 17.5 us  [key_turn(): needed = (base <= rows[-1]) & (base + row_count - 1 >= first[0])]
  transfers between devices with their start and end apart: 73 -> 87, of which waited for: 15 -> 30; matrix products, arithmetic and copies ran while one was open for 7% -> 10% of each run, Pallas kernels for 0% -> 0%
where the time goes in v1:
time: 1470 us; the launch traced here: 1460 us
  waiting for transfers between devices  705 us (48%)
  starting transfers between devices  271 us (18%)
  local copies, waits for them, and re-layouts  136 us (9%)
  other arithmetic  125 us (9%)
  matrix products  113 us (8%)
  blocking collectives  67.4 us (5%)
  loops' own time  22.9 us (2%)
  between operations  16.8 us (1%)
    psum x1, waiting for transfers between devices, shards(): lax.psum((grad_query_weight, grad_key_weight, grad_value_weight, grad_out...  513 us
    ppermute x32, starting transfers between devices, shifted(): return lax.ppermute(block, axis, route)  156 us
    psum x6, waiting for transfers between devices, head_sum(): return lax.psum(values.astype(jnp.bfloat16), 'tp').astype(jnp.float32)  131 us
    ppermute x32, starting transfers between devices, shifted_2(): lax.ppermute(value, axis, [(i, (i + by) % size) for i in range(size)])  82.9 us
    unnamed x231, local copies, waits for them, and re-layouts  72.8 us
    dot_general x30, matrix products, matmul(): return jnp.dot(left, right, preferred_element_type=jnp.float32)  70 us
    psum x1, blocking collectives, shards(): lax.psum((text_key_part.reshape(text_count, width_here), text_value_part....  67.4 us
    ppermute x8, waiting for transfers between devices, gather_around(): earlier.append(lax.ppermute(earlier[-1], axis, up))  37.5 us
  transfers between devices with their start and end apart: 87, of which 30 were waited for; matrix products, arithmetic and copies ran while one was open for 10% of the time, Pallas kernels for 0%

profile of v1, /device:TPU:0, one launch (start us, length us, event | category | flops | bytes accessed | tf_op | source)
XLA Modules:
  0.0 1457.6 jit_solution(5238895054559706508)
XLA Ops:
  15.1 9.0 collective-permute-done.4
  28.6 9.3 collective-permute-done.5
  53.8 6.8 collective-permute-done.7
  65.1 5.7 collective-permute-done.8
  73.9 4.7 collective-permute-start.16
  82.8 4.7 collective-permute-start.17
  134.6 75.3 %conditional.2 = (f32[256,8,64]{0,2,1:T(8,128)S(1)}, f32[8,256]{1,0:T(8,128)}, f32[8,256]{1,0:T(8,128)}, f32[8,256]{1,0:T(8,128)S(1)}) conditional(s32[]{:T(128)} %bitcast.10, () %tuple.66, (s32[4096]{0:T(1024)S(1)}, s32[4096]{0:T(1024)S(1)}, s32[256]{0:T(256)S(1)}, s32[256]{0:T(256)S(1)}, bf16[4096,512]{1,0:T(8,128)(2,1)}, ...), branch_computations={%region_5.6_spmd, %region_6.9_spmd.clone} | conditional | flops 2234513408 | bytes 147687616 | solution.py:176
  135.1 11.9 copy.81
  147.0 6.9 constant_dynamic-slice_fusion
  154.8 6.3 copy.80
  161.2 15.7 %select_reduce_fusion = (f32[8,256]{1,0:T(8,128)S(1)}, f32[8,256,4096]{2,1,0:T(8,128)}) fusion(pred[256,4096]{1,0:T(8,128)(4,1)S(1)} %compare_and_fusion.1, bf16[256,8,64]{0,2,1:T(8,128)(2,1)S(1)} %get-tuple-element.651, bf16[4096,8,64]{0,2,1:T(8,128)(2,1)} %bitcast.126), kind=kOutput, calls=%fused_computation.15 | convolution fusion | flops 1090516992 | bytes 39067648 | tf_op jit(solution)/shard_map/cond/branch_1_fun/qhd,khd->hqk/dot_general | solution.py:158
  177.4 15.6 %fusion.14 = f32[256,8,64]{0,2,1:T(8,128)S(1)} fusion(bf16[4096,8,64]{0,2,1:T(8,128)(2,1)} %bitcast.131, f32[8,256,4096]{2,1,0:T(8,128)} %get-tuple-element.911, f32[8,256]{1,0:T(8,128)} %broadcast_maximum_fusion, pred[256,4096]{1,0:T(8,128)(4,1)S(1)} %compare_and_fusion.1), kind=kOutput, calls=%fused_computation.21 | convolution fusion | flops 1107296256 | bytes 39329792 | tf_op jit(solution)/shard_map/cond/branch_1_fun/hqk,khd->qhd/dot_general | solution.py:166
  193.0 16.2 %fusion.9 = f32[8,256]{1,0:T(8,128)} fusion(f32[8,256,4096]{2,1,0:T(8,128)} %get-tuple-element.911, f32[8,256]{1,0:T(8,128)} %broadcast_maximum_fusion, pred[256,4096]{1,0:T(8,128)(4,1)S(1)} %compare_and_fusion.1), kind=kLoop, calls=%fused_computation.16 | loop fusion | flops 33552384 | bytes 34619392 | tf_op jit(solution)/shard_map/cond/branch_1_fun/reduce_sum | solution.py:165
  218.1 22.2 %all-reduce.12.cloned.1.call-done = bf16[256,1024]{1,0:T(8,128)(2,1)} async-done(((bf16[256,1024]{1,0:T(8,128)(2,1)}), bf16[256,1024]{1,0:T(8,128)(2,1)}) %all-reduce.12.cloned.1.call-update) | async-done | bytes 524304 | tf_op jit(solution)/shard_map/psum | solution.py:64
  254.7 25.3 %all-reduce.14.cloned.1.call-done = bf16[256,1024]{1,0:T(8,128)(2,1)} async-done(((bf16[256,1024]{1,0:T(8,128)(2,1)}), bf16[256,1024]{1,0:T(8,128)(2,1)}) %all-reduce.14.cloned.1.call-update) | async-done | bytes 524304 | tf_op jit(solution)/shard_map/psum | solution.py:64
  286.7 6.6 add_convert_fusion
  298.4 6.2 fusion.105
  306.7 4.8 fusion.85
  311.5 15.5 %all-reduce.16.cloned.1.call-done = bf16[256,1024]{1,0:T(8,128)(2,1)} async-done(((bf16[256,1024]{1,0:T(8,128)(2,1)}), bf16[256,1024]{1,0:T(8,128)(2,1)}) %all-reduce.16.cloned.1.call-update) | async-done | bytes 524304 | tf_op jit(solution)/shard_map/psum | solution.py:64
  345.0 24.9 %all-reduce.18.cloned.1.call-done = bf16[256,1024]{1,0:T(8,128)(2,1)} async-done(((bf16[256,1024]{1,0:T(8,128)(2,1)}), bf16[256,1024]{1,0:T(8,128)(2,1)}) %all-reduce.18.cloned.1.call-update) | async-done | bytes 524304 | tf_op jit(solution)/shard_map/psum | solution.py:64
  381.5 386.0 %while.26 = (s32[]{:T(128)}, bf16[256,512]{0,1:T(8,128)(2,1)S(1)}, bf16[256,512]{0,1:T(8,128)(2,1)S(1)}, f32[256,512]{0,1:T(8,128)}, f32[256,512]{0,1:T(8,128)},...) while((s32[]{:T(128)}, bf16[256,512]{0,1:T(8,128)(2,1)S(1)}, ...), condition=%wide.region_29.30_spmd.clone, body=%wide.region_26.29_spmd.clone.sunk | while | flops 341115168 | bytes 32471788 | solution.py:307
  384.8 6.0 conditional.5
  407.6 7.3 collective-permute-start.2
  434.4 8.4 collective-permute-start.3
  444.8 5.2 collective-permute-start.1
  462.0 8.6 collective-permute-start
  470.5 5.2 collective-permute-start.1
  490.2 11.2 collective-permute-start.1
  515.8 5.2 collective-permute-start.1
  537.8 5.2 collective-permute-start.1
  552.5 7.4 collective-permute-start.3
  563.5 5.2 collective-permute-start.1
  580.6 8.5 collective-permute-start
  589.1 5.2 collective-permute-start.1
  608.8 10.2 collective-permute-start.1
  634.5 5.2 collective-permute-start.1
  656.4 5.2 collective-permute-start.1
  672.3 5.2 collective-permute-start.3
  682.0 5.2 collective-permute-start.1
  699.2 8.5 collective-permute-start
  707.7 5.2 collective-permute-start.1
  727.4 9.2 collective-permute-start.1
  753.1 5.2 collective-permute-start.1
  758.3 5.7 collective-permute-done.2
  776.7 29.7 %all-reduce.20.cloned.1.call-done = bf16[256,1024]{1,0:T(8,128)(2,1)} async-done(((bf16[256,1024]{1,0:T(8,128)(2,1)}), bf16[256,1024]{1,0:T(8,128)(2,1)}) %all-reduce.20.cloned.1.call-update) | async-done | bytes 524304 | tf_op jit(solution)/shard_map/psum | solution.py:64
  810.0 67.4 %all-reduce.25 = (bf16[128,512]{0,1:T(8,128)(2,1)S(1)}, bf16[128,512]{0,1:T(8,128)(2,1)S(1)}, f32[1024]{0:T(1024)}, f32[1024]{0:T(1024)}, f32[1024]{0:T(1024)}, ...) all-reduce(f32[128,512]{0,1:T(8,128)S(1)} %bitcast.140, ...), channel_id=1, replica_groups=mesh['blk'=16,'tp'=2] {'blk'}, use_global_device_ids=true, to_apply=%region_33.34 | all-reduce | flops 137216 | bytes 835584 | tf_op jit(solution)/shard_map/psum | solution.py:241
  899.0 13.6 all-reduce.24.cloned.1.call-done
  916.4 512.8 %all-reduce.22.cloned.1.call-done = (f32[1024,512]{1,0:T(8,128)}, f32[1024,512]{1,0:T(8,128)}, f32[1024,512]{1,0:T(8,128)}, f32[512,1024]{1,0:T(8,128)}, f32[102...) async-done(((f32[1024,512]{1,0:T(8,128)}, f32[1024,512]{1,0:T(8,128)}, f32[1024,512]{1,0:T(8,128)}, f32[512,1024]{1,0:T(8,128)}, ...) | async-done | bytes 29360144 | tf_op jit(solution)/shard_map/psum | solution.py:341
  (658 shorter events, 429.4 us)
Async XLA Ops:
  7.3 127.3 %all-gather.2.cloned.1.call-start = ((), (), s32[]{:S(2)}) async-start(), calls=%async_computation | async-start | bytes 4456448 | tf_op jit(solution)/shard_map/all_gather | solution.py:149
  12.6 227.6 %all-reduce.12.cloned.1.call-start = ((), (), s32[]{:S(2)}) async-start(), calls=%async_computation.1 | async-start | bytes 1048576 | tf_op jit(solution)/shard_map/psum | solution.py:64
  24.1 13.7 collective-permute-start.5
  24.1 13.7 collective-permute-start.12
  46.5 14.1 collective-permute-start.7
  92.0 23.7 %collective-permute-start.18 = (bf16[256,512]{1,0:T(8,128)(2,1)}, bf16[256,512]{1,0:T(8,128)(2,1)S(1)}, u32[]{:S(2)}, u32[]{:S(2)}) collective-permute-start(bf16[256,512]{1,0:T(8,128)(2,1)} %collective-permute-done.17), channel_id=1, source_target_pairs={{0,30},{2,0},{4,2},{6,4},{8,6},{10,8},{12,10},{14,12},{16,14},{18,... | collective-permute-start | bytes 786440 | tf_op jit(solution)/shard_map/ppermute | solution.py:19
  213.5 66.5 %all-reduce.14.cloned.1.call-start = ((), (), s32[]{:S(2)}) async-start(), calls=%async_computation.2 | async-start | bytes 1048576 | tf_op jit(solution)/shard_map/psum | solution.py:64
  251.3 75.8 %all-reduce.16.cloned.1.call-start = ((), (), s32[]{:S(2)}) async-start(), calls=%async_computation.3 | async-start | bytes 1048576 | tf_op jit(solution)/shard_map/psum | solution.py:64
  298.3 71.6 %all-reduce.18.cloned.1.call-start = ((), (), s32[]{:S(2)}) async-start(), calls=%async_computation.4 | async-start | bytes 1048576 | tf_op jit(solution)/shard_map/psum | solution.py:64
  341.1 465.2 %all-reduce.20.cloned.1.call-start = ((), (), s32[]{:S(2)}) async-start(), calls=%async_computation.5 | async-start | bytes 1048576 | tf_op jit(solution)/shard_map/psum | solution.py:64
  407.6 16.8 %collective-permute-start.2 = (bf16[256,512]{0,1:T(8,128)(2,1)S(1)}, bf16[256,512]{0,1:T(8,128)(2,1)}, u32[]{:S(2)}, u32[]{:S(2)}) collective-permute-start(bf16[256,512]{0,1:T(8,128)(2,1)S(1)} %convert_element_type.504), channel_id=1, source_target_pairs={{0,2},{2,4},{4,6},{6,8},{8,10},{10,12},{12,14},{14,16},{16,18},{18... | collective-permute-start | bytes 786440 | tf_op jit(solution)/shard_map/while/body/eval_jaxpr/ppermute | solution.py:32
  431.5 18.6 %collective-permute-start.2 = (bf16[256,512]{0,1:T(8,128)(2,1)S(1)}, bf16[256,512]{0,1:T(8,128)(2,1)}, u32[]{:S(2)}, u32[]{:S(2)}) collective-permute-start(bf16[256,512]{0,1:T(8,128)(2,1)S(1)} %convert_element_type.504), channel_id=1, source_target_pairs={{0,2},{2,4},{4,6},{6,8},{8,10},{10,12},{12,14},{14,16},{16,18},{18... | collective-permute-start | bytes 786440 | tf_op jit(solution)/shard_map/while/body/eval_jaxpr/ppermute | solution.py:32
  434.4 17.4 %collective-permute-start.3 = (bf16[256,512]{0,1:T(8,128)(2,1)}, bf16[256,512]{0,1:T(8,128)(2,1)S(1)}, u32[]{:S(2)}, u32[]{:S(2)}) collective-permute-start(bf16[256,512]{0,1:T(8,128)(2,1)} %convert_element_type.506), channel_id=1, source_target_pairs={{0,2},{2,4},{4,6},{6,8},{8,10},{10,12},{12,14},{14,16},{16,18},{18... | collective-permute-start | bytes 786440 | tf_op jit(solution)/shard_map/while/body/eval_jaxpr/ppermute | solution.py:32
  457.1 18.6 %collective-permute-start.2 = (bf16[256,512]{0,1:T(8,128)(2,1)S(1)}, bf16[256,512]{0,1:T(8,128)(2,1)}, u32[]{:S(2)}, u32[]{:S(2)}) collective-permute-start(bf16[256,512]{0,1:T(8,128)(2,1)S(1)} %convert_element_type.504), channel_id=1, source_target_pairs={{0,2},{2,4},{4,6},{6,8},{8,10},{10,12},{12,14},{14,16},{16,18},{18... | collective-permute-start | bytes 786440 | tf_op jit(solution)/shard_map/while/body/eval_jaxpr/ppermute | solution.py:32
  459.6 17.9 %collective-permute-start.3 = (bf16[256,512]{0,1:T(8,128)(2,1)}, bf16[256,512]{0,1:T(8,128)(2,1)S(1)}, u32[]{:S(2)}, u32[]{:S(2)}) collective-permute-start(bf16[256,512]{0,1:T(8,128)(2,1)} %convert_element_type.506), channel_id=1, source_target_pairs={{0,2},{2,4},{4,6},{6,8},{8,10},{10,12},{12,14},{14,16},{16,18},{18... | collective-permute-start | bytes 786440 | tf_op jit(solution)/shard_map/while/body/eval_jaxpr/ppermute | solution.py:32
  462.0 16.4 %collective-permute-start = (bf16[256,512]{0,1:T(8,128)(2,1)S(1)}, bf16[256,512]{0,1:T(8,128)(2,1)S(1)}, u32[]{:S(2)}, u32[]{:S(2)}) collective-permute-start(bf16[256,512]{0,1:T(8,128)(2,1)S(1)} %copy.157), channel_id=1, source_target_pairs={{0,2},{2,4},{4,6},{6,8},{8,10},{10,12},{12,14},{14,16},{16,18},{18... | collective-permute-start | bytes 786440 | tf_op jit(solution)/shard_map/while/body/eval_jaxpr/ppermute | solution.py:27
  482.8 18.6 %collective-permute-start.2 = (bf16[256,512]{0,1:T(8,128)(2,1)S(1)}, bf16[256,512]{0,1:T(8,128)(2,1)}, u32[]{:S(2)}, u32[]{:S(2)}) collective-permute-start(bf16[256,512]{0,1:T(8,128)(2,1)S(1)} %convert_element_type.504), channel_id=1, source_target_pairs={{0,2},{2,4},{4,6},{6,8},{8,10},{10,12},{12,14},{14,16},{16,18},{18... | collective-permute-start | bytes 786440 | tf_op jit(solution)/shard_map/while/body/eval_jaxpr/ppermute | solution.py:32
  485.3 17.9 %collective-permute-start.3 = (bf16[256,512]{0,1:T(8,128)(2,1)}, bf16[256,512]{0,1:T(8,128)(2,1)S(1)}, u32[]{:S(2)}, u32[]{:S(2)}) collective-permute-start(bf16[256,512]{0,1:T(8,128)(2,1)} %convert_element_type.506), channel_id=1, source_target_pairs={{0,2},{2,4},{4,6},{6,8},{8,10},{10,12},{12,14},{14,16},{16,18},{18... | collective-permute-start | bytes 786440 | tf_op jit(solution)/shard_map/while/body/eval_jaxpr/ppermute | solution.py:32
  487.6 16.4 %collective-permute-start = (bf16[256,512]{0,1:T(8,128)(2,1)S(1)}, bf16[256,512]{0,1:T(8,128)(2,1)S(1)}, u32[]{:S(2)}, u32[]{:S(2)}) collective-permute-start(bf16[256,512]{0,1:T(8,128)(2,1)S(1)} %copy.157), channel_id=1, source_target_pairs={{0,2},{2,4},{4,6},{6,8},{8,10},{10,12},{12,14},{14,16},{16,18},{18... | collective-permute-start | bytes 786440 | tf_op jit(solution)/shard_map/while/body/eval_jaxpr/ppermute | solution.py:27
  490.2 13.8 collective-permute-start.1
  528.2 14.8 %collective-permute-start.2 = (bf16[256,512]{0,1:T(8,128)(2,1)S(1)}, bf16[256,512]{0,1:T(8,128)(2,1)}, u32[]{:S(2)}, u32[]{:S(2)}) collective-permute-start(bf16[256,512]{0,1:T(8,128)(2,1)S(1)} %convert_element_type.504), channel_id=1, source_target_pairs={{0,2},{2,4},{4,6},{6,8},{8,10},{10,12},{12,14},{14,16},{16,18},{18... | collective-permute-start | bytes 786440 | tf_op jit(solution)/shard_map/while/body/eval_jaxpr/ppermute | solution.py:32
  550.1 18.6 %collective-permute-start.2 = (bf16[256,512]{0,1:T(8,128)(2,1)S(1)}, bf16[256,512]{0,1:T(8,128)(2,1)}, u32[]{:S(2)}, u32[]{:S(2)}) collective-permute-start(bf16[256,512]{0,1:T(8,128)(2,1)S(1)} %convert_element_type.504), channel_id=1, source_target_pairs={{0,2},{2,4},{4,6},{6,8},{8,10},{10,12},{12,14},{14,16},{16,18},{18... | collective-permute-start | bytes 786440 | tf_op jit(solution)/shard_map/while/body/eval_jaxpr/ppermute | solution.py:32
  552.5 17.9 %collective-permute-start.3 = (bf16[256,512]{0,1:T(8,128)(2,1)}, bf16[256,512]{0,1:T(8,128)(2,1)S(1)}, u32[]{:S(2)}, u32[]{:S(2)}) collective-permute-start(bf16[256,512]{0,1:T(8,128)(2,1)} %convert_element_type.506), channel_id=1, source_target_pairs={{0,2},{2,4},{4,6},{6,8},{8,10},{10,12},{12,14},{14,16},{16,18},{18... | collective-permute-start | bytes 786440 | tf_op jit(solution)/shard_map/while/body/eval_jaxpr/ppermute | solution.py:32
  575.8 18.5 %collective-permute-start.2 = (bf16[256,512]{0,1:T(8,128)(2,1)S(1)}, bf16[256,512]{0,1:T(8,128)(2,1)}, u32[]{:S(2)}, u32[]{:S(2)}) collective-permute-start(bf16[256,512]{0,1:T(8,128)(2,1)S(1)} %convert_element_type.504), channel_id=1, source_target_pairs={{0,2},{2,4},{4,6},{6,8},{8,10},{10,12},{12,14},{14,16},{16,18},{18... | collective-permute-start | bytes 786440 | tf_op jit(solution)/shard_map/while/body/eval_jaxpr/ppermute | solution.py:32
  578.2 17.9 %collective-permute-start.3 = (bf16[256,512]{0,1:T(8,128)(2,1)}, bf16[256,512]{0,1:T(8,128)(2,1)S(1)}, u32[]{:S(2)}, u32[]{:S(2)}) collective-permute-start(bf16[256,512]{0,1:T(8,128)(2,1)} %convert_element_type.506), channel_id=1, source_target_pairs={{0,2},{2,4},{4,6},{6,8},{8,10},{10,12},{12,14},{14,16},{16,18},{18... | collective-permute-start | bytes 786440 | tf_op jit(solution)/shard_map/while/body/eval_jaxpr/ppermute | solution.py:32
  580.6 16.3 %collective-permute-start = (bf16[256,512]{0,1:T(8,128)(2,1)S(1)}, bf16[256,512]{0,1:T(8,128)(2,1)S(1)}, u32[]{:S(2)}, u32[]{:S(2)}) collective-permute-start(bf16[256,512]{0,1:T(8,128)(2,1)S(1)} %copy.157), channel_id=1, source_target_pairs={{0,2},{2,4},{4,6},{6,8},{8,10},{10,12},{12,14},{14,16},{16,18},{18... | collective-permute-start | bytes 786440 | tf_op jit(solution)/shard_map/while/body/eval_jaxpr/ppermute | solution.py:27
  601.4 17.6 %collective-permute-start.2 = (bf16[256,512]{0,1:T(8,128)(2,1)S(1)}, bf16[256,512]{0,1:T(8,128)(2,1)}, u32[]{:S(2)}, u32[]{:S(2)}) collective-permute-start(bf16[256,512]{0,1:T(8,128)(2,1)S(1)} %convert_element_type.504), channel_id=1, source_target_pairs={{0,2},{2,4},{4,6},{6,8},{8,10},{10,12},{12,14},{14,16},{16,18},{18... | collective-permute-start | bytes 786440 | tf_op jit(solution)/shard_map/while/body/eval_jaxpr/ppermute | solution.py:32
  603.8 16.9 %collective-permute-start.3 = (bf16[256,512]{0,1:T(8,128)(2,1)}, bf16[256,512]{0,1:T(8,128)(2,1)S(1)}, u32[]{:S(2)}, u32[]{:S(2)}) collective-permute-start(bf16[256,512]{0,1:T(8,128)(2,1)} %convert_element_type.506), channel_id=1, source_target_pairs={{0,2},{2,4},{4,6},{6,8},{8,10},{10,12},{12,14},{14,16},{16,18},{18... | collective-permute-start | bytes 786440 | tf_op jit(solution)/shard_map/while/body/eval_jaxpr/ppermute | solution.py:32
  606.2 15.4 %collective-permute-start = (bf16[256,512]{0,1:T(8,128)(2,1)S(1)}, bf16[256,512]{0,1:T(8,128)(2,1)S(1)}, u32[]{:S(2)}, u32[]{:S(2)}) collective-permute-start(bf16[256,512]{0,1:T(8,128)(2,1)S(1)} %copy.157), channel_id=1, source_target_pairs={{0,2},{2,4},{4,6},{6,8},{8,10},{10,12},{12,14},{14,16},{16,18},{18... | collective-permute-start | bytes 786440 | tf_op jit(solution)/shard_map/while/body/eval_jaxpr/ppermute | solution.py:27
  626.1 13.6 collective-permute-start.2
  646.8 16.7 %collective-permute-start.2 = (bf16[256,512]{0,1:T(8,128)(2,1)S(1)}, bf16[256,512]{0,1:T(8,128)(2,1)}, u32[]{:S(2)}, u32[]{:S(2)}) collective-permute-start(bf16[256,512]{0,1:T(8,128)(2,1)S(1)} %convert_element_type.504), channel_id=1, source_target_pairs={{0,2},{2,4},{4,6},{6,8},{8,10},{10,12},{12,14},{14,16},{16,18},{18... | collective-permute-start | bytes 786440 | tf_op jit(solution)/shard_map/while/body/eval_jaxpr/ppermute | solution.py:32
  651.4 14.8 %collective-permute-start.3 = (bf16[256,512]{0,1:T(8,128)(2,1)}, bf16[256,512]{0,1:T(8,128)(2,1)S(1)}, u32[]{:S(2)}, u32[]{:S(2)}) collective-permute-start(bf16[256,512]{0,1:T(8,128)(2,1)} %convert_element_type.506), channel_id=1, source_target_pairs={{0,2},{2,4},{4,6},{6,8},{8,10},{10,12},{12,14},{14,16},{16,18},{18... | collective-permute-start | bytes 786440 | tf_op jit(solution)/shard_map/while/body/eval_jaxpr/ppermute | solution.py:32
  671.5 16.7 %collective-permute-start.2 = (bf16[256,512]{0,1:T(8,128)(2,1)S(1)}, bf16[256,512]{0,1:T(8,128)(2,1)}, u32[]{:S(2)}, u32[]{:S(2)}) collective-permute-start(bf16[256,512]{0,1:T(8,128)(2,1)S(1)} %convert_element_type.504), channel_id=1, source_target_pairs={{0,2},{2,4},{4,6},{6,8},{8,10},{10,12},{12,14},{14,16},{16,18},{18... | collective-permute-start | bytes 786440 | tf_op jit(solution)/shard_map/while/body/eval_jaxpr/ppermute | solution.py:32
  672.3 18.6 %collective-permute-start.3 = (bf16[256,512]{0,1:T(8,128)(2,1)}, bf16[256,512]{0,1:T(8,128)(2,1)S(1)}, u32[]{:S(2)}, u32[]{:S(2)}) collective-permute-start(bf16[256,512]{0,1:T(8,128)(2,1)} %convert_element_type.506), channel_id=1, source_target_pairs={{0,2},{2,4},{4,6},{6,8},{8,10},{10,12},{12,14},{14,16},{16,18},{18... | collective-permute-start | bytes 786440 | tf_op jit(solution)/shard_map/while/body/eval_jaxpr/ppermute | solution.py:32
  677.5 14.3 collective-permute-start
  696.3 16.7 %collective-permute-start.2 = (bf16[256,512]{0,1:T(8,128)(2,1)S(1)}, bf16[256,512]{0,1:T(8,128)(2,1)}, u32[]{:S(2)}, u32[]{:S(2)}) collective-permute-start(bf16[256,512]{0,1:T(8,128)(2,1)S(1)} %convert_element_type.504), channel_id=1, source_target_pairs={{0,2},{2,4},{4,6},{6,8},{8,10},{10,12},{12,14},{14,16},{16,18},{18... | collective-permute-start | bytes 786440 | tf_op jit(solution)/shard_map/while/body/eval_jaxpr/ppermute | solution.py:32
  697.1 18.6 %collective-permute-start.3 = (bf16[256,512]{0,1:T(8,128)(2,1)}, bf16[256,512]{0,1:T(8,128)(2,1)S(1)}, u32[]{:S(2)}, u32[]{:S(2)}) collective-permute-start(bf16[256,512]{0,1:T(8,128)(2,1)} %convert_element_type.506), channel_id=1, source_target_pairs={{0,2},{2,4},{4,6},{6,8},{8,10},{10,12},{12,14},{14,16},{16,18},{18... | collective-permute-start | bytes 786440 | tf_op jit(solution)/shard_map/while/body/eval_jaxpr/ppermute | solution.py:32
  699.2 17.4 %collective-permute-start = (bf16[256,512]{0,1:T(8,128)(2,1)S(1)}, bf16[256,512]{0,1:T(8,128)(2,1)S(1)}, u32[]{:S(2)}, u32[]{:S(2)}) collective-permute-start(bf16[256,512]{0,1:T(8,128)(2,1)S(1)} %copy.157), channel_id=1, source_target_pairs={{0,2},{2,4},{4,6},{6,8},{8,10},{10,12},{12,14},{14,16},{16,18},{18... | collective-permute-start | bytes 786440 | tf_op jit(solution)/shard_map/while/body/eval_jaxpr/ppermute | solution.py:27
  721.0 17.3 %collective-permute-start.2 = (bf16[256,512]{0,1:T(8,128)(2,1)S(1)}, bf16[256,512]{0,1:T(8,128)(2,1)}, u32[]{:S(2)}, u32[]{:S(2)}) collective-permute-start(bf16[256,512]{0,1:T(8,128)(2,1)S(1)} %convert_element_type.504), channel_id=1, source_target_pairs={{0,2},{2,4},{4,6},{6,8},{8,10},{10,12},{12,14},{14,16},{16,18},{18... | collective-permute-start | bytes 786440 | tf_op jit(solution)/shard_map/while/body/eval_jaxpr/ppermute | solution.py:32
  722.4 18.6 %collective-permute-start.3 = (bf16[256,512]{0,1:T(8,128)(2,1)}, bf16[256,512]{0,1:T(8,128)(2,1)S(1)}, u32[]{:S(2)}, u32[]{:S(2)}) collective-permute-start(bf16[256,512]{0,1:T(8,128)(2,1)} %convert_element_type.506), channel_id=1, source_target_pairs={{0,2},{2,4},{4,6},{6,8},{8,10},{10,12},{12,14},{14,16},{16,18},{18... | collective-permute-start | bytes 786440 | tf_op jit(solution)/shard_map/while/body/eval_jaxpr/ppermute | solution.py:32
  724.8 17.0 %collective-permute-start = (bf16[256,512]{0,1:T(8,128)(2,1)S(1)}, bf16[256,512]{0,1:T(8,128)(2,1)S(1)}, u32[]{:S(2)}, u32[]{:S(2)}) collective-permute-start(bf16[256,512]{0,1:T(8,128)(2,1)S(1)} %copy.157), channel_id=1, source_target_pairs={{0,2},{2,4},{4,6},{6,8},{8,10},{10,12},{12,14},{14,16},{16,18},{18... | collective-permute-start | bytes 786440 | tf_op jit(solution)/shard_map/while/body/eval_jaxpr/ppermute | solution.py:27
  727.4 14.4 collective-permute-start.1
  746.3 17.6 %collective-permute-start.2 = (bf16[256,512]{0,1:T(8,128)(2,1)S(1)}, bf16[256,512]{0,1:T(8,128)(2,1)}, u32[]{:S(2)}, u32[]{:S(2)}) collective-permute-start(bf16[256,512]{0,1:T(8,128)(2,1)S(1)} %convert_element_type.504), channel_id=1, source_target_pairs={{0,2},{2,4},{4,6},{6,8},{8,10},{10,12},{12,14},{14,16},{16,18},{18... | collective-permute-start | bytes 786440 | tf_op jit(solution)/shard_map/while/body/eval_jaxpr/ppermute | solution.py:32
  748.1 18.6 %collective-permute-start.3 = (bf16[256,512]{0,1:T(8,128)(2,1)}, bf16[256,512]{0,1:T(8,128)(2,1)S(1)}, u32[]{:S(2)}, u32[]{:S(2)}) collective-permute-start(bf16[256,512]{0,1:T(8,128)(2,1)} %convert_element_type.506), channel_id=1, source_target_pairs={{0,2},{2,4},{4,6},{6,8},{8,10},{10,12},{12,14},{14,16},{16,18},{18... | collective-permute-start | bytes 786440 | tf_op jit(solution)/shard_map/while/body/eval_jaxpr/ppermute | solution.py:32
  750.5 17.0 %collective-permute-start = (bf16[256,512]{0,1:T(8,128)(2,1)S(1)}, bf16[256,512]{0,1:T(8,128)(2,1)S(1)}, u32[]{:S(2)}, u32[]{:S(2)}) collective-permute-start(bf16[256,512]{0,1:T(8,128)(2,1)S(1)} %copy.157), channel_id=1, source_target_pairs={{0,2},{2,4},{4,6},{6,8},{8,10},{10,12},{12,14},{14,16},{16,18},{18... | collective-permute-start | bytes 786440 | tf_op jit(solution)/shard_map/while/body/eval_jaxpr/ppermute | solution.py:27
  753.1 14.4 collective-permute-start.1
  772.9 139.7 %all-reduce.24.cloned.1.call-start = ((), (), s32[]{:S(2)}) async-start(), calls=%async_computation.7 | async-start | bytes 1572864 | tf_op jit(solution)/shard_map/psum | solution.py:64
  881.6 547.5 %all-reduce.22.cloned.1.call-start = ((), (), s32[]{:S(2)}) async-start(), calls=%async_computation.6 | async-start | bytes 58720256 | tf_op jit(solution)/shard_map/psum | solution.py:341
  (135 other events, 2234.1 us)
Sparse Core Ops, SparseCore 0:
  12.7 67.3 all-gather.1
  213.7 26.5 all-reduce.11
  251.4 28.5 all-reduce.13
  298.4 28.5 all-reduce.15
  341.3 28.5 all-reduce.17
  773.0 33.2 all-reduce.19
  881.7 30.8 all-reduce.23
  919.6 509.5 all-reduce.21
